TPU v7x, 32 devices: a whole 2x2x4 slice. The times are simulated.
32 devices in a mesh: row: 8 (over y, x, core), col: 4 (over z).
Axes of the slice: x: 2, y: 2, z: 4, core: 2. Of those that a mesh axis runs over, the one named last changes fastest.
Arguments:
- a_panels: bfloat16 [16384, 1024], P('row', 'col'), may hold values from -6 to 6
- a_mask: int32 [128, 8], P('row', 'col'), may hold values 0 or 1
- b_panels: bfloat16 [1024, 4096], P('row', 'col'), may hold values from -0.1875 to 0.1875
- b_mask: int32 [8, 32], P('row', 'col'), may hold values 0 or 1
- owner_map: int32 [128, 1], P('row'), may hold values from 0 to 7; in each aligned block of 16 rows (0 to 15, 16 to 31, ...) at most 2 rows name the same one
Outputs:
- owned: bfloat16 [16384, 4096], P('row', 'col')
Inputs may be any that keep to these rules, and one draw needn't show every extreme that they name: `owner_map`: within each aligned block of 16 tile rows (the tile rows of one grid row) no owner is named more than 2 times, a bound that some block reaches.
All inputs are finite; a program needn't handle non-finite values. No bound on the sum of `a_mask` or of `b_mask` on one device may be relied on, other than what follows from the above.
Results may differ from a plain program's by a relative error of at most 0.001.
Values may be sent and summed in bfloat16 or wider, within the bound.
No kernel may reach another device: no remote copies, remote signals or barrier semaphores. Data moves between devices by JAX's collectives and lax.ppermute only.
A program may use at most 128 MiB of HBM per device.

v0:
```python
import jax
import jax.numpy as jnp
from jax import lax
from jax.sharding import PartitionSpec as P

SLOTS = 2


def from_behind(value, axis, steps):
    count = lax.axis_size(axis)
    pairs = [(source, (source + steps) % count) for source in range(count)]
    return lax.ppermute(value, axis, pairs)


def masked_a(panel, mask):
    tile_rows = mask.shape[0]
    inner = mask.shape[1]
    tiles = panel.reshape(tile_rows, panel.shape[0] // tile_rows, inner, panel.shape[1] // inner)
    return (tiles * mask.astype(jnp.bfloat16)[:, None, :, None]).reshape(panel.shape)


def masked_b(panel, mask):
    inner = mask.shape[0]
    tile_cols = mask.shape[1]
    tiles = panel.reshape(inner, panel.shape[0] // inner, tile_cols, panel.shape[1] // tile_cols)
    return (tiles * mask.astype(jnp.bfloat16)[:, None, :, None]).reshape(panel.shape)


def product(panel_a, mask_a, panel_b, mask_b):
    return jnp.dot(
        masked_a(panel_a, mask_a), masked_b(panel_b, mask_b), preferred_element_type=jnp.float32
    )


def on_device(a_panels, a_mask, b_panels, b_mask, owner_map):
    tile = b_panels.shape[0]
    depth = lax.axis_size("col")
    grid_rows = lax.axis_size("row")
    fold = grid_rows // depth
    row_id = lax.axis_index("row")
    col_id = lax.axis_index("col")
    panel_b, mask_b = (b_panels, b_mask)
    target = fold * col_id
    for bit in range((grid_rows - 1).bit_length()):
        moved_b, moved_bm = from_behind((panel_b, mask_b), "row", -(1 << bit))
        take = target >> bit & 1 == 1
        panel_b = jnp.where(take, moved_b, panel_b)
        mask_b = jnp.where(take, moved_bm, mask_b)
    total = jnp.zeros((a_panels.shape[0], b_panels.shape[1]), jnp.float32)
    panel_a, mask_a = (a_panels, a_mask)
    whole_shift = row_id // fold
    remain = row_id % fold
    for bit in range((depth - 1).bit_length()):
        moved_a, moved_am = from_behind((panel_a, mask_a), "col", -(1 << bit))
        take = whole_shift >> bit & 1 == 1
        panel_a = jnp.where(take, moved_a, panel_a)
        mask_a = jnp.where(take, moved_am, mask_a)
    after_a, after_am = from_behind((panel_a, mask_a), "col", -1)
    joined = jnp.concatenate([panel_a, after_a], axis=1)
    joined_m = jnp.concatenate([mask_a, after_am], axis=1)
    panel_a = lax.dynamic_slice_in_dim(joined, remain * tile, fold * tile, 1)
    mask_a = lax.dynamic_slice_in_dim(joined_m, remain, fold, 1)

    def advance(step, carry):
        acc, cur_a, cur_am, cur_b, cur_bm = carry
        acc = acc + product(cur_a[:, :tile], cur_am[:, :1], cur_b, cur_bm)
        head_a, head_m = from_behind((cur_a[:, :tile], cur_am[:, :1]), "col", -1)
        cur_a = jnp.concatenate([cur_a[:, tile:], head_a], axis=1)
        cur_am = jnp.concatenate([cur_am[:, 1:], head_m], axis=1)
        cur_b, cur_bm = from_behind((cur_b, cur_bm), "row", -1)
        return (acc, cur_a, cur_am, cur_b, cur_bm)

    total, panel_a, mask_a, panel_b, mask_b = lax.fori_loop(
        0, grid_rows - 1, advance, (total, panel_a, mask_a, panel_b, mask_b)
    )
    total = total + product(panel_a[:, :tile], mask_a[:, :1], panel_b, mask_b)
    result = total.astype(jnp.bfloat16)
    owners = owner_map[:, 0]
    tile_rows = owners.shape[0]
    same = owners[:, None] == owners[None, :]
    earlier = (
        jnp.arange(tile_rows, dtype=jnp.int32)[None, :]
        < jnp.arange(tile_rows, dtype=jnp.int32)[:, None]
    )
    rank = jnp.sum(jnp.where(same & earlier, 1, 0).astype(jnp.int32), axis=1)
    slot_id = owners * SLOTS + rank
    select = (jnp.arange(grid_rows * SLOTS, dtype=jnp.int32)[:, None] == slot_id[None, :]).astype(
        jnp.bfloat16
    )
    packed = jnp.dot(
        select, result.reshape(tile_rows, -1), preferred_element_type=jnp.float32
    ).astype(jnp.bfloat16)
    packed = packed.reshape(grid_rows, SLOTS * tile, result.shape[1])
    arrived = lax.all_to_all(packed, "row", split_axis=0, concat_axis=0, tiled=True)
    return arrived.reshape(-1, result.shape[1])


def solution(mesh):
    placed = (P("row", "col"), P("row", "col"), P("row", "col"), P("row", "col"), P("row", None))
    return jax.shard_map(
        on_device, mesh=mesh, in_specs=placed, out_specs=P("row", "col"), check_vma=False
    )
```

profile of v0, /device:TPU:0, one launch (start us, length us, event | category | flops | bytes accessed | tf_op | source)
XLA Modules:
  0.0 282.8 jit_solution(3299915901711081954)
XLA Ops:
  0.0 5.0 %collective-permute-start.4 = (bf16[2048,256]{1,0:T(8,128)(2,1)}, bf16[2048,256]{1,0:T(8,128)(2,1)S(1)}, u32[]{:S(2)}, u32[]{:S(2)}) collective-permute-start(bf16[2048,256]{1,0:T(8,128)(2,1)} %param.7), channel_id=1, source_target_pairs={{0,3},{1,0},{2,1},{3,2},{4,7},{5,4},{6,5},{7,6},{8,11},{9,8},{10,9... | collective-permute-start | bytes 3145736 | tf_op jit(solution)/shard_map/ppermute | solution.py:12
  5.5 1.3 collective-permute-start.10
  6.8 1.2 collective-permute-start.13
  8.1 0.9 select_reduce_fusion
  9.0 18.8 %collective-permute-done.4 = bf16[2048,256]{1,0:T(8,128)(2,1)S(1)} collective-permute-done((bf16[2048,256]{1,0:T(8,128)(2,1)}, bf16[2048,256]{1,0:T(8,128)(2,1)S(1)}, u32[]{:S(2)}, u32[]{:S(2)}) %collective-permute-start.4) | collective-permute-done | bytes 1048608 | tf_op jit(solution)/shard_map/ppermute | solution.py:12
  27.8 1.3 broadcast_select_fusion
  29.1 1.4 collective-permute-start.5
  31.2 0.7 broadcast_select_fusion.5
  31.9 1.2 collective-permute-start.14
  33.1 2.3 collective-permute-done.14
  35.4 1.5 collective-permute-start.15
  37.0 0.7 broadcast_select_fusion.8
  37.6 1.6 collective-permute-start.8
  39.2 1.0 broadcast_select_fusion.2
  40.7 35.9 %collective-permute-done.5 = bf16[2048,256]{1,0:T(8,128)(2,1)S(1)} collective-permute-done((bf16[2048,256]{1,0:T(8,128)(2,1)S(1)}, bf16[2048,256]{1,0:T(8,128)(2,1)S(1)}, u32[]{:S(2)}, u32[]{:S(2)}) %collective-permute-start.5) | collective-permute-done | bytes 1048608 | tf_op jit(solution)/shard_map/ppermute | solution.py:12
  76.7 2.3 collective-permute-start.6
  79.2 1.6 collective-permute-start.12
  80.8 20.9 %collective-permute-done.9 = s32[16,2]{0,1:T(2,128)S(1)} collective-permute-done((s32[16,2]{0,1:T(2,128)S(1)}, s32[16,2]{0,1:T(2,128)S(1)}, u32[]{:S(2)}, u32[]{:S(2)}) %collective-permute-start.9) | collective-permute-done | bytes 160 | tf_op jit(solution)/shard_map/ppermute | solution.py:12
  102.2 96.9 %while.19 = (s32[]{:T(128)}, f32[2048,1024]{1,0:T(8,128)}, bf16[2048,256]{1,0:T(8,128)(2,1)S(1)}, s32[16,2]{0,1:T(2,128)S(1)}, bf16[128,1024]{1,0:T(8,128)(2,1)S...) while((s32[]{:T(128)}, f32[2048,1024]{1,0:T(8,128)}, bf16[2048,256]{1,0:T(8,128)(2,1)S(1)}, ...), condition=%wide.region_2.3_spmd.clone, body=%wide.region_1.2_spmd.clone.sunk | while | flops 543555584 | bytes 25441596 | solution.py:73
  102.2 4.4 %collective-permute-start = (bf16[2048,128]{1,0:T(8,128)(2,1)S(1)}, bf16[2048,128]{1,0:T(8,128)(2,1)S(1)}, u32[]{:S(2)}, u32[]{:S(2)}) collective-permute-start(bf16[2048,128]{1,0:T(8,128)(2,1)S(1)} %get-tuple-element.127), channel_id=1, source_target_pairs={{0,3},{1,0},{2,1},{3,2},{4,7},{5,4},{6,5},{7,6},{8,11},{9,8},{10,9... | collective-permute-start | bytes 1572872 | tf_op jit(solution)/shard_map/while/body/eval_jaxpr/ppermute | solution.py:12
  106.8 1.3 collective-permute-start.3
  108.2 4.5 %select_add_fusion.2 = f32[2048,1024]{1,0:T(8,128)} fusion(f32[2048,1024]{1,0:T(8,128)} %get-tuple-element.140, pred[]{:T(512)S(6)} %compare.6, bf16[128,1024]{1,0:T(8,128)(2,1)S(1)} %copy.16, bf16[2048]{0:T(1024)(128)(2,1)S(1)} %broadcast_bitcast_fusion.6, bf16[1024]{0:T(1024)(128)(2,1)S(1)} %broadcast_bitcast_fusion.7, ...), kind=kOutput, calls=%fused_computation.clone.1 | convolution fusion | flops 541458432 | bytes 17569792 | tf_op jit(solution)/shard_map/while/body/eval_jaxpr/dot_general | solution.py:30
  112.8 4.3 %collective-permute-done.1 = s32[16,1]{0,1:T(1,128)S(1)} collective-permute-done((s32[16,1]{0,1:T(1,128)S(1)}, s32[16,1]{0,1:T(1,128)S(1)}, u32[]{:S(2)}, u32[]{:S(2)}) %collective-permute-start.1) | collective-permute-done | bytes 96 | tf_op jit(solution)/shard_map/while/body/eval_jaxpr/ppermute | solution.py:12
  117.4 4.4 %collective-permute-start = (bf16[2048,128]{1,0:T(8,128)(2,1)S(1)}, bf16[2048,128]{1,0:T(8,128)(2,1)S(1)}, u32[]{:S(2)}, u32[]{:S(2)}) collective-permute-start(bf16[2048,128]{1,0:T(8,128)(2,1)S(1)} %get-tuple-element.127), channel_id=1, source_target_pairs={{0,3},{1,0},{2,1},{3,2},{4,7},{5,4},{6,5},{7,6},{8,11},{9,8},{10,9... | collective-permute-start | bytes 1572872 | tf_op jit(solution)/shard_map/while/body/eval_jaxpr/ppermute | solution.py:12
  121.9 1.3 collective-permute-start.3
  123.3 7.9 %select_add_fusion.2 = f32[2048,1024]{1,0:T(8,128)} fusion(f32[2048,1024]{1,0:T(8,128)} %get-tuple-element.140, pred[]{:T(512)S(6)} %compare.6, bf16[128,1024]{1,0:T(8,128)(2,1)S(1)} %copy.16, bf16[2048]{0:T(1024)(128)(2,1)S(1)} %broadcast_bitcast_fusion.6, bf16[1024]{0:T(1024)(128)(2,1)S(1)} %broadcast_bitcast_fusion.7, ...), kind=kOutput, calls=%fused_computation.clone.1 | convolution fusion | flops 541458432 | bytes 17569792 | tf_op jit(solution)/shard_map/while/body/eval_jaxpr/dot_general | solution.py:30
  131.5 4.3 %collective-permute-start = (bf16[2048,128]{1,0:T(8,128)(2,1)S(1)}, bf16[2048,128]{1,0:T(8,128)(2,1)S(1)}, u32[]{:S(2)}, u32[]{:S(2)}) collective-permute-start(bf16[2048,128]{1,0:T(8,128)(2,1)S(1)} %get-tuple-element.127), channel_id=1, source_target_pairs={{0,3},{1,0},{2,1},{3,2},{4,7},{5,4},{6,5},{7,6},{8,11},{9,8},{10,9... | collective-permute-start | bytes 1572872 | tf_op jit(solution)/shard_map/while/body/eval_jaxpr/ppermute | solution.py:12
  136.0 1.3 collective-permute-start.3
  137.5 7.9 %select_add_fusion.2 = f32[2048,1024]{1,0:T(8,128)} fusion(f32[2048,1024]{1,0:T(8,128)} %get-tuple-element.140, pred[]{:T(512)S(6)} %compare.6, bf16[128,1024]{1,0:T(8,128)(2,1)S(1)} %copy.16, bf16[2048]{0:T(1024)(128)(2,1)S(1)} %broadcast_bitcast_fusion.6, bf16[1024]{0:T(1024)(128)(2,1)S(1)} %broadcast_bitcast_fusion.7, ...), kind=kOutput, calls=%fused_computation.clone.1 | convolution fusion | flops 541458432 | bytes 17569792 | tf_op jit(solution)/shard_map/while/body/eval_jaxpr/dot_general | solution.py:30
  145.7 3.3 %collective-permute-start = (bf16[2048,128]{1,0:T(8,128)(2,1)S(1)}, bf16[2048,128]{1,0:T(8,128)(2,1)S(1)}, u32[]{:S(2)}, u32[]{:S(2)}) collective-permute-start(bf16[2048,128]{1,0:T(8,128)(2,1)S(1)} %get-tuple-element.127), channel_id=1, source_target_pairs={{0,3},{1,0},{2,1},{3,2},{4,7},{5,4},{6,5},{7,6},{8,11},{9,8},{10,9... | collective-permute-start | bytes 1572872 | tf_op jit(solution)/shard_map/while/body/eval_jaxpr/ppermute | solution.py:12
  149.1 1.3 collective-permute-start.3
  150.6 7.9 %select_add_fusion.2 = f32[2048,1024]{1,0:T(8,128)} fusion(f32[2048,1024]{1,0:T(8,128)} %get-tuple-element.140, pred[]{:T(512)S(6)} %compare.6, bf16[128,1024]{1,0:T(8,128)(2,1)S(1)} %copy.16, bf16[2048]{0:T(1024)(128)(2,1)S(1)} %broadcast_bitcast_fusion.6, bf16[1024]{0:T(1024)(128)(2,1)S(1)} %broadcast_bitcast_fusion.7, ...), kind=kOutput, calls=%fused_computation.clone.1 | convolution fusion | flops 541458432 | bytes 17569792 | tf_op jit(solution)/shard_map/while/body/eval_jaxpr/dot_general | solution.py:30
  159.3 2.2 collective-permute-start
  161.7 1.8 collective-permute-start.3
  163.7 7.9 %select_add_fusion.2 = f32[2048,1024]{1,0:T(8,128)} fusion(f32[2048,1024]{1,0:T(8,128)} %get-tuple-element.140, pred[]{:T(512)S(6)} %compare.6, bf16[128,1024]{1,0:T(8,128)(2,1)S(1)} %copy.16, bf16[2048]{0:T(1024)(128)(2,1)S(1)} %broadcast_bitcast_fusion.6, bf16[1024]{0:T(1024)(128)(2,1)S(1)} %broadcast_bitcast_fusion.7, ...), kind=kOutput, calls=%fused_computation.clone.1 | convolution fusion | flops 541458432 | bytes 17569792 | tf_op jit(solution)/shard_map/while/body/eval_jaxpr/dot_general | solution.py:30
  172.4 3.2 %collective-permute-start = (bf16[2048,128]{1,0:T(8,128)(2,1)S(1)}, bf16[2048,128]{1,0:T(8,128)(2,1)S(1)}, u32[]{:S(2)}, u32[]{:S(2)}) collective-permute-start(bf16[2048,128]{1,0:T(8,128)(2,1)S(1)} %get-tuple-element.127), channel_id=1, source_target_pairs={{0,3},{1,0},{2,1},{3,2},{4,7},{5,4},{6,5},{7,6},{8,11},{9,8},{10,9... | collective-permute-start | bytes 1572872 | tf_op jit(solution)/shard_map/while/body/eval_jaxpr/ppermute | solution.py:12
  175.8 1.9 collective-permute-start.3
  177.8 7.9 %select_add_fusion.2 = f32[2048,1024]{1,0:T(8,128)} fusion(f32[2048,1024]{1,0:T(8,128)} %get-tuple-element.140, pred[]{:T(512)S(6)} %compare.6, bf16[128,1024]{1,0:T(8,128)(2,1)S(1)} %copy.16, bf16[2048]{0:T(1024)(128)(2,1)S(1)} %broadcast_bitcast_fusion.6, bf16[1024]{0:T(1024)(128)(2,1)S(1)} %broadcast_bitcast_fusion.7, ...), kind=kOutput, calls=%fused_computation.clone.1 | convolution fusion | flops 541458432 | bytes 17569792 | tf_op jit(solution)/shard_map/while/body/eval_jaxpr/dot_general | solution.py:30
  186.0 3.1 %collective-permute-start = (bf16[2048,128]{1,0:T(8,128)(2,1)S(1)}, bf16[2048,128]{1,0:T(8,128)(2,1)S(1)}, u32[]{:S(2)}, u32[]{:S(2)}) collective-permute-start(bf16[2048,128]{1,0:T(8,128)(2,1)S(1)} %get-tuple-element.127), channel_id=1, source_target_pairs={{0,3},{1,0},{2,1},{3,2},{4,7},{5,4},{6,5},{7,6},{8,11},{9,8},{10,9... | collective-permute-start | bytes 1572872 | tf_op jit(solution)/shard_map/while/body/eval_jaxpr/ppermute | solution.py:12
  189.3 1.5 collective-permute-start.3
  190.9 7.9 %select_add_fusion.2 = f32[2048,1024]{1,0:T(8,128)} fusion(f32[2048,1024]{1,0:T(8,128)} %get-tuple-element.140, pred[]{:T(512)S(6)} %compare.6, bf16[128,1024]{1,0:T(8,128)(2,1)S(1)} %copy.16, bf16[2048]{0:T(1024)(128)(2,1)S(1)} %broadcast_bitcast_fusion.6, bf16[1024]{0:T(1024)(128)(2,1)S(1)} %broadcast_bitcast_fusion.7, ...), kind=kOutput, calls=%fused_computation.clone.1 | convolution fusion | flops 541458432 | bytes 17569792 | tf_op jit(solution)/shard_map/while/body/eval_jaxpr/dot_general | solution.py:30
  199.2 4.6 %fusion.6 = f32[2048,1024]{1,0:T(8,128)} fusion(bf16[2048,256]{1,0:T(8,128)(2,1)S(1)} %get-tuple-element.42, bf16[128,1024]{1,0:T(8,128)(2,1)S(1)} %get-tuple-element.44, bf16[2048]{0:T(1024)(128)(2,1)S(1)} %broadcast_bitcast_fusion.2, bf16[1024]{0:T(1024)(128)(2,1)S(1)} %broadcast_bitcast_fusion.3), kind=kOutput, calls=%fused_computation.19 | convolution fusion | flops 537264128 | bytes 9181184 | tf_op jit(solution)/shard_map/dot_general | solution.py:30
  203.8 9.3 %add_convert_fusion = bf16[2048,1024]{1,0:T(8,128)(2,1)} fusion(f32[2048,1024]{1,0:T(8,128)} %get-tuple-element.41, f32[2048,1024]{1,0:T(8,128)} %fusion.6), kind=kLoop, calls=%fused_computation.13 | loop fusion | flops 4194304 | bytes 20971520 | tf_op jit(solution)/shard_map/convert_element_type | solution.py:77
  213.1 4.8 %reshape.54 = bf16[16,131072]{1,0:T(8,128)(2,1)} reshape(bf16[2048,1024]{1,0:T(8,128)(2,1)} %add_convert_fusion) | data formatting | bytes 8388608 | tf_op jit(solution)/shard_map/reshape | solution.py:91
  217.9 5.4 %convolution_convert_fusion = bf16[16,131072]{1,0:T(8,128)(2,1)} fusion(bf16[16,131072]{1,0:T(8,128)(2,1)} %reshape.54, s32[16]{0:T(128)S(1)} %multiply_add_fusion), kind=kOutput, calls=%fused_computation.12 | convolution fusion | flops 69206272 | bytes 8388672 | tf_op jit(solution)/shard_map/dot_general | solution.py:90
  223.3 4.8 %reshape.55 = bf16[8,256,1024]{2,1,0:T(8,128)(2,1)} reshape(bf16[16,131072]{1,0:T(8,128)(2,1)} %convolution_convert_fusion) | data formatting | bytes 8388608 | tf_op jit(solution)/shard_map/reshape | solution.py:93
  228.2 52.7 %all_to_all.5 = bf16[8,256,1024]{2,1,0:T(8,128)(2,1)S(1)} all-to-all(bf16[8,256,1024]{2,1,0:T(8,128)(2,1)} %reshape.55), channel_id=1, replica_groups=mesh['row'=8,'col'=4] {'row'}, dimensions={0} | all-to-all | bytes 8388608 | tf_op jit(solution)/shard_map/all_to_all | solution.py:94
  280.8 2.0 copy.25
  (131 shorter events, 7.2 us)
Async XLA Ops:
  0.0 27.8 %collective-permute-start.4 = (bf16[2048,256]{1,0:T(8,128)(2,1)}, bf16[2048,256]{1,0:T(8,128)(2,1)S(1)}, u32[]{:S(2)}, u32[]{:S(2)}) collective-permute-start(bf16[2048,256]{1,0:T(8,128)(2,1)} %param.7), channel_id=1, source_target_pairs={{0,3},{1,0},{2,1},{3,2},{4,7},{5,4},{6,5},{7,6},{8,11},{9,8},{10,9... | collective-permute-start | bytes 3145736 | tf_op jit(solution)/shard_map/ppermute | solution.py:12
  5.0 31.9 %collective-permute-start.7 = (s32[16,2]{0,1:T(2,128)}, s32[16,2]{0,1:T(2,128)S(1)}, u32[]{:S(2)}, u32[]{:S(2)}) collective-permute-start(s32[16,2]{0,1:T(2,128)} %param.8), channel_id=1, source_target_pairs={{0,3},{1,0},{2,1},{3,2},{4,7},{5,4},{6,5},{7,6},{8,11},{9,8},{10,9... | collective-permute-start | bytes 392 | tf_op jit(solution)/shard_map/ppermute | solution.py:12
  5.5 33.7 %collective-permute-start.10 = (bf16[128,1024]{1,0:T(8,128)(2,1)}, bf16[128,1024]{1,0:T(8,128)(2,1)S(1)}, u32[]{:S(2)}, u32[]{:S(2)}) collective-permute-start(bf16[128,1024]{1,0:T(8,128)(2,1)} %param.9), channel_id=1, source_target_pairs={{0,28},{4,0},{8,4},{12,8},{16,12},{20,16},{24,20},{28,24},{1,29},{... | collective-permute-start | bytes 786440 | tf_op jit(solution)/shard_map/ppermute | solution.py:12
  6.8 24.4 %collective-permute-start.13 = (s32[1,8]{1,0:T(1,128)}, s32[1,8]{1,0:T(1,128)S(1)}, u32[]{:S(2)}, u32[]{:S(2)}) collective-permute-start(s32[1,8]{1,0:T(1,128)} %param.10), channel_id=1, source_target_pairs={{0,28},{4,0},{8,4},{12,8},{16,12},{20,16},{24,20},{28,24},{1,29},{... | collective-permute-start | bytes 104 | tf_op jit(solution)/shard_map/ppermute | solution.py:12
  29.1 47.5 %collective-permute-start.5 = (bf16[2048,256]{1,0:T(8,128)(2,1)S(1)}, bf16[2048,256]{1,0:T(8,128)(2,1)S(1)}, u32[]{:S(2)}, u32[]{:S(2)}) collective-permute-start(bf16[2048,256]{1,0:T(8,128)(2,1)S(1)} %broadcast_select_fusion), channel_id=1, source_target_pairs={{0,2},{1,3},{2,0},{3,1},{4,6},{5,7},{6,4},{7,5},{8,10},{9,11},{10,... | collective-permute-start | bytes 3145736 | tf_op jit(solution)/shard_map/ppermute | solution.py:12
  31.9 3.5 %collective-permute-start.14 = (s32[1,8]{1,0:T(1,128)S(1)}, s32[1,8]{1,0:T(1,128)S(1)}, u32[]{:S(2)}, u32[]{:S(2)}) collective-permute-start(s32[1,8]{1,0:T(1,128)S(1)} %broadcast_select_fusion.5), channel_id=1, source_target_pairs={{0,24},{4,28},{8,0},{12,4},{16,8},{20,12},{24,16},{28,20},{1,25},{... | collective-permute-start | bytes 104 | tf_op jit(solution)/shard_map/ppermute | solution.py:12
  35.4 45.3 %collective-permute-start.15 = (s32[1,8]{1,0:T(1,128)S(1)}, s32[1,8]{1,0:T(1,128)S(1)}, u32[]{:S(2)}, u32[]{:S(2)}) collective-permute-start(s32[1,8]{1,0:T(1,128)S(1)} %broadcast_select_fusion.6), channel_id=1, source_target_pairs={{0,16},{4,20},{8,24},{12,28},{16,0},{20,4},{24,8},{28,12},{1,17},{... | collective-permute-start | bytes 104 | tf_op jit(solution)/shard_map/ppermute | solution.py:12
  37.6 41.4 %collective-permute-start.8 = (s32[16,2]{0,1:T(2,128)S(1)}, s32[16,2]{0,1:T(2,128)S(1)}, u32[]{:S(2)}, u32[]{:S(2)}) collective-permute-start(s32[16,2]{0,1:T(2,128)S(1)} %broadcast_select_fusion.8), channel_id=1, source_target_pairs={{0,2},{1,3},{2,0},{3,1},{4,6},{5,7},{6,4},{7,5},{8,10},{9,11},{10,... | collective-permute-start | bytes 392 | tf_op jit(solution)/shard_map/ppermute | solution.py:12
  40.2 39.0 %collective-permute-start.11 = (bf16[128,1024]{1,0:T(8,128)(2,1)S(1)}, bf16[128,1024]{1,0:T(8,128)(2,1)S(1)}, u32[]{:S(2)}, u32[]{:S(2)}) collective-permute-start(bf16[128,1024]{1,0:T(8,128)(2,1)S(1)} %broadcast_select_fusion.2), channel_id=1, source_target_pairs={{0,24},{4,28},{8,0},{12,4},{16,8},{20,12},{24,16},{28,20},{1,25},{... | collective-permute-start | bytes 786440 | tf_op jit(solution)/shard_map/ppermute | solution.py:12
  76.7 25.0 %collective-permute-start.6 = (bf16[2048,256]{1,0:T(8,128)(2,1)S(1)}, bf16[2048,256]{1,0:T(8,128)(2,1)S(1)}, u32[]{:S(2)}, u32[]{:S(2)}) collective-permute-start(bf16[2048,256]{1,0:T(8,128)(2,1)S(1)} %broadcast_select_fusion.1), channel_id=1, source_target_pairs={{0,3},{1,0},{2,1},{3,2},{4,7},{5,4},{6,5},{7,6},{8,11},{9,8},{10,9... | collective-permute-start | bytes 3145736 | tf_op jit(solution)/shard_map/ppermute | solution.py:12
  79.1 22.6 %collective-permute-start.9 = (s32[16,2]{0,1:T(2,128)S(1)}, s32[16,2]{0,1:T(2,128)S(1)}, u32[]{:S(2)}, u32[]{:S(2)}) collective-permute-start(s32[16,2]{0,1:T(2,128)S(1)} %broadcast_select_fusion.9), channel_id=1, source_target_pairs={{0,3},{1,0},{2,1},{3,2},{4,7},{5,4},{6,5},{7,6},{8,11},{9,8},{10,9... | collective-permute-start | bytes 392 | tf_op jit(solution)/shard_map/ppermute | solution.py:12
  79.2 22.5 %collective-permute-start.12 = (bf16[128,1024]{1,0:T(8,128)(2,1)S(1)}, bf16[128,1024]{1,0:T(8,128)(2,1)S(1)}, u32[]{:S(2)}, u32[]{:S(2)}) collective-permute-start(bf16[128,1024]{1,0:T(8,128)(2,1)S(1)} %broadcast_select_fusion.3), channel_id=1, source_target_pairs={{0,16},{4,20},{8,24},{12,28},{16,0},{20,4},{24,8},{28,12},{1,17},{... | collective-permute-start | bytes 786440 | tf_op jit(solution)/shard_map/ppermute | solution.py:12
  102.2 14.9 %collective-permute-start = (bf16[2048,128]{1,0:T(8,128)(2,1)S(1)}, bf16[2048,128]{1,0:T(8,128)(2,1)S(1)}, u32[]{:S(2)}, u32[]{:S(2)}) collective-permute-start(bf16[2048,128]{1,0:T(8,128)(2,1)S(1)} %get-tuple-element.127), channel_id=1, source_target_pairs={{0,3},{1,0},{2,1},{3,2},{4,7},{5,4},{6,5},{7,6},{8,11},{9,8},{10,9... | collective-permute-start | bytes 1572872 | tf_op jit(solution)/shard_map/while/body/eval_jaxpr/ppermute | solution.py:12
  106.6 10.5 %collective-permute-start.1 = (s32[16,1]{0,1:T(1,128)S(1)}, s32[16,1]{0,1:T(1,128)S(1)}, u32[]{:S(2)}, u32[]{:S(2)}) collective-permute-start(s32[16,1]{0,1:T(1,128)S(1)} %get-tuple-element.129), channel_id=1, source_target_pairs={{0,3},{1,0},{2,1},{3,2},{4,7},{5,4},{6,5},{7,6},{8,11},{9,8},{10,9... | collective-permute-start | bytes 200 | tf_op jit(solution)/shard_map/while/body/eval_jaxpr/ppermute | solution.py:12
  106.7 10.6 %collective-permute-start.2 = (bf16[128,1024]{1,0:T(8,128)(2,1)S(1)}, bf16[128,1024]{1,0:T(8,128)(2,1)S(1)}, u32[]{:S(2)}, u32[]{:S(2)}) collective-permute-start(bf16[128,1024]{1,0:T(8,128)(2,1)S(1)} %copy.16), channel_id=1, source_target_pairs={{0,28},{4,0},{8,4},{12,8},{16,12},{20,16},{24,20},{28,24},{1,29},{... | collective-permute-start | bytes 786440 | tf_op jit(solution)/shard_map/while/body/eval_jaxpr/ppermute | solution.py:12
  106.8 10.5 %collective-permute-start.3 = (s32[1,8]{1,0:T(1,128)S(1)}, s32[1,8]{1,0:T(1,128)S(1)}, u32[]{:S(2)}, u32[]{:S(2)}) collective-permute-start(s32[1,8]{1,0:T(1,128)S(1)} %copy.17), channel_id=1, source_target_pairs={{0,28},{4,0},{8,4},{12,8},{16,12},{20,16},{24,20},{28,24},{1,29},{... | collective-permute-start | bytes 104 | tf_op jit(solution)/shard_map/while/body/eval_jaxpr/ppermute | solution.py:12
  117.4 13.9 %collective-permute-start = (bf16[2048,128]{1,0:T(8,128)(2,1)S(1)}, bf16[2048,128]{1,0:T(8,128)(2,1)S(1)}, u32[]{:S(2)}, u32[]{:S(2)}) collective-permute-start(bf16[2048,128]{1,0:T(8,128)(2,1)S(1)} %get-tuple-element.127), channel_id=1, source_target_pairs={{0,3},{1,0},{2,1},{3,2},{4,7},{5,4},{6,5},{7,6},{8,11},{9,8},{10,9... | collective-permute-start | bytes 1572872 | tf_op jit(solution)/shard_map/while/body/eval_jaxpr/ppermute | solution.py:12
  121.7 9.6 %collective-permute-start.1 = (s32[16,1]{0,1:T(1,128)S(1)}, s32[16,1]{0,1:T(1,128)S(1)}, u32[]{:S(2)}, u32[]{:S(2)}) collective-permute-start(s32[16,1]{0,1:T(1,128)S(1)} %get-tuple-element.129), channel_id=1, source_target_pairs={{0,3},{1,0},{2,1},{3,2},{4,7},{5,4},{6,5},{7,6},{8,11},{9,8},{10,9... | collective-permute-start | bytes 200 | tf_op jit(solution)/shard_map/while/body/eval_jaxpr/ppermute | solution.py:12
  121.8 9.6 %collective-permute-start.2 = (bf16[128,1024]{1,0:T(8,128)(2,1)S(1)}, bf16[128,1024]{1,0:T(8,128)(2,1)S(1)}, u32[]{:S(2)}, u32[]{:S(2)}) collective-permute-start(bf16[128,1024]{1,0:T(8,128)(2,1)S(1)} %copy.16), channel_id=1, source_target_pairs={{0,28},{4,0},{8,4},{12,8},{16,12},{20,16},{24,20},{28,24},{1,29},{... | collective-permute-start | bytes 786440 | tf_op jit(solution)/shard_map/while/body/eval_jaxpr/ppermute | solution.py:12
  121.9 9.5 %collective-permute-start.3 = (s32[1,8]{1,0:T(1,128)S(1)}, s32[1,8]{1,0:T(1,128)S(1)}, u32[]{:S(2)}, u32[]{:S(2)}) collective-permute-start(s32[1,8]{1,0:T(1,128)S(1)} %copy.17), channel_id=1, source_target_pairs={{0,28},{4,0},{8,4},{12,8},{16,12},{20,16},{24,20},{28,24},{1,29},{... | collective-permute-start | bytes 104 | tf_op jit(solution)/shard_map/while/body/eval_jaxpr/ppermute | solution.py:12
  131.5 13.9 %collective-permute-start = (bf16[2048,128]{1,0:T(8,128)(2,1)S(1)}, bf16[2048,128]{1,0:T(8,128)(2,1)S(1)}, u32[]{:S(2)}, u32[]{:S(2)}) collective-permute-start(bf16[2048,128]{1,0:T(8,128)(2,1)S(1)} %get-tuple-element.127), channel_id=1, source_target_pairs={{0,3},{1,0},{2,1},{3,2},{4,7},{5,4},{6,5},{7,6},{8,11},{9,8},{10,9... | collective-permute-start | bytes 1572872 | tf_op jit(solution)/shard_map/while/body/eval_jaxpr/ppermute | solution.py:12
  135.8 9.6 %collective-permute-start.1 = (s32[16,1]{0,1:T(1,128)S(1)}, s32[16,1]{0,1:T(1,128)S(1)}, u32[]{:S(2)}, u32[]{:S(2)}) collective-permute-start(s32[16,1]{0,1:T(1,128)S(1)} %get-tuple-element.129), channel_id=1, source_target_pairs={{0,3},{1,0},{2,1},{3,2},{4,7},{5,4},{6,5},{7,6},{8,11},{9,8},{10,9... | collective-permute-start | bytes 200 | tf_op jit(solution)/shard_map/while/body/eval_jaxpr/ppermute | solution.py:12
  135.9 9.6 %collective-permute-start.2 = (bf16[128,1024]{1,0:T(8,128)(2,1)S(1)}, bf16[128,1024]{1,0:T(8,128)(2,1)S(1)}, u32[]{:S(2)}, u32[]{:S(2)}) collective-permute-start(bf16[128,1024]{1,0:T(8,128)(2,1)S(1)} %copy.16), channel_id=1, source_target_pairs={{0,28},{4,0},{8,4},{12,8},{16,12},{20,16},{24,20},{28,24},{1,29},{... | collective-permute-start | bytes 786440 | tf_op jit(solution)/shard_map/while/body/eval_jaxpr/ppermute | solution.py:12
  136.0 9.5 %collective-permute-start.3 = (s32[1,8]{1,0:T(1,128)S(1)}, s32[1,8]{1,0:T(1,128)S(1)}, u32[]{:S(2)}, u32[]{:S(2)}) collective-permute-start(s32[1,8]{1,0:T(1,128)S(1)} %copy.17), channel_id=1, source_target_pairs={{0,28},{4,0},{8,4},{12,8},{16,12},{20,16},{24,20},{28,24},{1,29},{... | collective-permute-start | bytes 104 | tf_op jit(solution)/shard_map/while/body/eval_jaxpr/ppermute | solution.py:12
  145.7 13.4 %collective-permute-start = (bf16[2048,128]{1,0:T(8,128)(2,1)S(1)}, bf16[2048,128]{1,0:T(8,128)(2,1)S(1)}, u32[]{:S(2)}, u32[]{:S(2)}) collective-permute-start(bf16[2048,128]{1,0:T(8,128)(2,1)S(1)} %get-tuple-element.127), channel_id=1, source_target_pairs={{0,3},{1,0},{2,1},{3,2},{4,7},{5,4},{6,5},{7,6},{8,11},{9,8},{10,9... | collective-permute-start | bytes 1572872 | tf_op jit(solution)/shard_map/while/body/eval_jaxpr/ppermute | solution.py:12
  149.0 10.1 %collective-permute-start.1 = (s32[16,1]{0,1:T(1,128)S(1)}, s32[16,1]{0,1:T(1,128)S(1)}, u32[]{:S(2)}, u32[]{:S(2)}) collective-permute-start(s32[16,1]{0,1:T(1,128)S(1)} %get-tuple-element.129), channel_id=1, source_target_pairs={{0,3},{1,0},{2,1},{3,2},{4,7},{5,4},{6,5},{7,6},{8,11},{9,8},{10,9... | collective-permute-start | bytes 200 | tf_op jit(solution)/shard_map/while/body/eval_jaxpr/ppermute | solution.py:12
  149.1 10.2 %collective-permute-start.2 = (bf16[128,1024]{1,0:T(8,128)(2,1)S(1)}, bf16[128,1024]{1,0:T(8,128)(2,1)S(1)}, u32[]{:S(2)}, u32[]{:S(2)}) collective-permute-start(bf16[128,1024]{1,0:T(8,128)(2,1)S(1)} %copy.16), channel_id=1, source_target_pairs={{0,28},{4,0},{8,4},{12,8},{16,12},{20,16},{24,20},{28,24},{1,29},{... | collective-permute-start | bytes 786440 | tf_op jit(solution)/shard_map/while/body/eval_jaxpr/ppermute | solution.py:12
  149.1 10.1 %collective-permute-start.3 = (s32[1,8]{1,0:T(1,128)S(1)}, s32[1,8]{1,0:T(1,128)S(1)}, u32[]{:S(2)}, u32[]{:S(2)}) collective-permute-start(s32[1,8]{1,0:T(1,128)S(1)} %copy.17), channel_id=1, source_target_pairs={{0,28},{4,0},{8,4},{12,8},{16,12},{20,16},{24,20},{28,24},{1,29},{... | collective-permute-start | bytes 104 | tf_op jit(solution)/shard_map/while/body/eval_jaxpr/ppermute | solution.py:12
  159.3 12.9 %collective-permute-start = (bf16[2048,128]{1,0:T(8,128)(2,1)S(1)}, bf16[2048,128]{1,0:T(8,128)(2,1)S(1)}, u32[]{:S(2)}, u32[]{:S(2)}) collective-permute-start(bf16[2048,128]{1,0:T(8,128)(2,1)S(1)} %get-tuple-element.127), channel_id=1, source_target_pairs={{0,3},{1,0},{2,1},{3,2},{4,7},{5,4},{6,5},{7,6},{8,11},{9,8},{10,9... | collective-permute-start | bytes 1572872 | tf_op jit(solution)/shard_map/while/body/eval_jaxpr/ppermute | solution.py:12
  161.5 10.7 %collective-permute-start.1 = (s32[16,1]{0,1:T(1,128)S(1)}, s32[16,1]{0,1:T(1,128)S(1)}, u32[]{:S(2)}, u32[]{:S(2)}) collective-permute-start(s32[16,1]{0,1:T(1,128)S(1)} %get-tuple-element.129), channel_id=1, source_target_pairs={{0,3},{1,0},{2,1},{3,2},{4,7},{5,4},{6,5},{7,6},{8,11},{9,8},{10,9... | collective-permute-start | bytes 200 | tf_op jit(solution)/shard_map/while/body/eval_jaxpr/ppermute | solution.py:12
  161.6 10.7 %collective-permute-start.2 = (bf16[128,1024]{1,0:T(8,128)(2,1)S(1)}, bf16[128,1024]{1,0:T(8,128)(2,1)S(1)}, u32[]{:S(2)}, u32[]{:S(2)}) collective-permute-start(bf16[128,1024]{1,0:T(8,128)(2,1)S(1)} %copy.16), channel_id=1, source_target_pairs={{0,28},{4,0},{8,4},{12,8},{16,12},{20,16},{24,20},{28,24},{1,29},{... | collective-permute-start | bytes 786440 | tf_op jit(solution)/shard_map/while/body/eval_jaxpr/ppermute | solution.py:12
  161.7 10.6 %collective-permute-start.3 = (s32[1,8]{1,0:T(1,128)S(1)}, s32[1,8]{1,0:T(1,128)S(1)}, u32[]{:S(2)}, u32[]{:S(2)}) collective-permute-start(s32[1,8]{1,0:T(1,128)S(1)} %copy.17), channel_id=1, source_target_pairs={{0,28},{4,0},{8,4},{12,8},{16,12},{20,16},{24,20},{28,24},{1,29},{... | collective-permute-start | bytes 104 | tf_op jit(solution)/shard_map/while/body/eval_jaxpr/ppermute | solution.py:12
  172.4 13.3 %collective-permute-start = (bf16[2048,128]{1,0:T(8,128)(2,1)S(1)}, bf16[2048,128]{1,0:T(8,128)(2,1)S(1)}, u32[]{:S(2)}, u32[]{:S(2)}) collective-permute-start(bf16[2048,128]{1,0:T(8,128)(2,1)S(1)} %get-tuple-element.127), channel_id=1, source_target_pairs={{0,3},{1,0},{2,1},{3,2},{4,7},{5,4},{6,5},{7,6},{8,11},{9,8},{10,9... | collective-permute-start | bytes 1572872 | tf_op jit(solution)/shard_map/while/body/eval_jaxpr/ppermute | solution.py:12
  175.6 10.1 %collective-permute-start.1 = (s32[16,1]{0,1:T(1,128)S(1)}, s32[16,1]{0,1:T(1,128)S(1)}, u32[]{:S(2)}, u32[]{:S(2)}) collective-permute-start(s32[16,1]{0,1:T(1,128)S(1)} %get-tuple-element.129), channel_id=1, source_target_pairs={{0,3},{1,0},{2,1},{3,2},{4,7},{5,4},{6,5},{7,6},{8,11},{9,8},{10,9... | collective-permute-start | bytes 200 | tf_op jit(solution)/shard_map/while/body/eval_jaxpr/ppermute | solution.py:12
  175.7 10.2 %collective-permute-start.2 = (bf16[128,1024]{1,0:T(8,128)(2,1)S(1)}, bf16[128,1024]{1,0:T(8,128)(2,1)S(1)}, u32[]{:S(2)}, u32[]{:S(2)}) collective-permute-start(bf16[128,1024]{1,0:T(8,128)(2,1)S(1)} %copy.16), channel_id=1, source_target_pairs={{0,28},{4,0},{8,4},{12,8},{16,12},{20,16},{24,20},{28,24},{1,29},{... | collective-permute-start | bytes 786440 | tf_op jit(solution)/shard_map/while/body/eval_jaxpr/ppermute | solution.py:12
  175.8 10.1 %collective-permute-start.3 = (s32[1,8]{1,0:T(1,128)S(1)}, s32[1,8]{1,0:T(1,128)S(1)}, u32[]{:S(2)}, u32[]{:S(2)}) collective-permute-start(s32[1,8]{1,0:T(1,128)S(1)} %copy.17), channel_id=1, source_target_pairs={{0,28},{4,0},{8,4},{12,8},{16,12},{20,16},{24,20},{28,24},{1,29},{... | collective-permute-start | bytes 104 | tf_op jit(solution)/shard_map/while/body/eval_jaxpr/ppermute | solution.py:12
  186.0 12.9 %collective-permute-start = (bf16[2048,128]{1,0:T(8,128)(2,1)S(1)}, bf16[2048,128]{1,0:T(8,128)(2,1)S(1)}, u32[]{:S(2)}, u32[]{:S(2)}) collective-permute-start(bf16[2048,128]{1,0:T(8,128)(2,1)S(1)} %get-tuple-element.127), channel_id=1, source_target_pairs={{0,3},{1,0},{2,1},{3,2},{4,7},{5,4},{6,5},{7,6},{8,11},{9,8},{10,9... | collective-permute-start | bytes 1572872 | tf_op jit(solution)/shard_map/while/body/eval_jaxpr/ppermute | solution.py:12
  189.1 9.8 %collective-permute-start.1 = (s32[16,1]{0,1:T(1,128)S(1)}, s32[16,1]{0,1:T(1,128)S(1)}, u32[]{:S(2)}, u32[]{:S(2)}) collective-permute-start(s32[16,1]{0,1:T(1,128)S(1)} %get-tuple-element.129), channel_id=1, source_target_pairs={{0,3},{1,0},{2,1},{3,2},{4,7},{5,4},{6,5},{7,6},{8,11},{9,8},{10,9... | collective-permute-start | bytes 200 | tf_op jit(solution)/shard_map/while/body/eval_jaxpr/ppermute | solution.py:12
  189.2 9.8 %collective-permute-start.2 = (bf16[128,1024]{1,0:T(8,128)(2,1)S(1)}, bf16[128,1024]{1,0:T(8,128)(2,1)S(1)}, u32[]{:S(2)}, u32[]{:S(2)}) collective-permute-start(bf16[128,1024]{1,0:T(8,128)(2,1)S(1)} %copy.16), channel_id=1, source_target_pairs={{0,28},{4,0},{8,4},{12,8},{16,12},{20,16},{24,20},{28,24},{1,29},{... | collective-permute-start | bytes 786440 | tf_op jit(solution)/shard_map/while/body/eval_jaxpr/ppermute | solution.py:12
  189.3 9.8 %collective-permute-start.3 = (s32[1,8]{1,0:T(1,128)S(1)}, s32[1,8]{1,0:T(1,128)S(1)}, u32[]{:S(2)}, u32[]{:S(2)}) collective-permute-start(s32[1,8]{1,0:T(1,128)S(1)} %copy.17), channel_id=1, source_target_pairs={{0,28},{4,0},{8,4},{12,8},{16,12},{20,16},{24,20},{28,24},{1,29},{... | collective-permute-start | bytes 104 | tf_op jit(solution)/shard_map/while/body/eval_jaxpr/ppermute | solution.py:12
where the time goes:
time: 283 us
  waiting for transfers between devices  83.4 us (29%)
  matrix products  62.1 us (22%)
  starting transfers between devices  54.5 us (19%)
  blocking collectives  52.7 us (19%)
  other arithmetic  16 us (6%)
  local copies, waits for them, and re-layouts  13.5 us (5%)
    ppermute x40, waiting for transfers between devices, from_behind(): return lax.ppermute(value, axis, pairs)  83.4 us
    dot_general x8, matrix products, product(): jnp.dot(masked_a(panel_a, mask_a), masked_b(panel_b, mask_b), preferred_e...  56.6 us
    ppermute x40, starting transfers between devices, from_behind(): return lax.ppermute(value, axis, pairs)  54.5 us
    all_to_all x1, blocking collectives, on_device(): lax.all_to_all(packed, 'row', split_axis=0, concat_axis=0, tiled=True)  52.7 us
    convert_element_type x1, other arithmetic, on_device(): result = total.astype(jnp.bfloat16)  9.3 us
  transfers between devices with their start and end apart: 40, of which 7 were waited for; matrix products, arithmetic and copies ran while one was open for 21% of the time, Pallas kernels for 0%

commit v1 on v0

--- a/solution.py
+++ b/solution.py
@@ -91,7 +91,19 @@
         select, result.reshape(tile_rows, -1), preferred_element_type=jnp.float32
     ).astype(jnp.bfloat16)
     packed = packed.reshape(grid_rows, SLOTS * tile, result.shape[1])
-    arrived = lax.all_to_all(packed, "row", split_axis=0, concat_axis=0, tiled=True)
+    ways, here = (lax.axis_size("row"), lax.axis_index("row"))
+    width = packed.shape[0] // ways
+    shape = list(packed.shape)
+    shape[0] = width
+    height = shape[0]
+    shape[0] = height * ways
+    full = jnp.zeros(shape, packed.dtype)
+    for mask_2 in range(ways):
+        part = lax.dynamic_slice_in_dim(packed, (here ^ mask_2) * width, width, axis=0)
+        if mask_2:
+            part = lax.ppermute(part, "row", [(d, d ^ mask_2) for d in range(ways)])
+        full = lax.dynamic_update_slice_in_dim(full, part, (here ^ mask_2) * height, axis=0)
+    arrived = full
     return arrived.reshape(-1, result.shape[1])
 
 

time: 283 us -> 283 us (level)
  blocking collectives: 52.7 us -> 0 us
  waiting for transfers between devices: 83.4 us -> 126 us
  starting transfers between devices: 54.5 us -> 60.4 us
  local copies, waits for them, and re-layouts: 13.5 us -> 16.4 us
    all_to_all x1 -> x0, blocking collectives: 52.7 us -> none  [on_device(): lax.all_to_all(packed, 'row', split_axis=0, concat_axis=0, tiled=True)]
    ppermute x0 -> x7, waiting for transfers between devices: none -> 43.1 us  [on_device(): part = lax.ppermute(part, 'row', [(d, d ^ mask_2) for d in range(ways)])]
    ppermute x0 -> x7, starting transfers between devices: none -> 5.94 us  [on_device(): part = lax.ppermute(part, 'row', [(d, d ^ mask_2) for d in range(ways)])]
  transfers between devices with their start and end apart: 40 -> 47, of which waited for: 7 -> 10; matrix products, arithmetic and copies ran while one was open for 21% -> 21% of each run, Pallas kernels for 0% -> 0%
where the time goes in v1:
time: 283 us; the launch traced here: 282 us
  waiting for transfers between devices  126 us (45%)
  matrix products  62.3 us (22%)
  starting transfers between devices  60.4 us (21%)
  local copies, waits for them, and re-layouts  16.4 us (6%)
  other arithmetic  16 us (6%)
    ppermute x40, waiting for transfers between devices, from_behind(): return lax.ppermute(value, axis, pairs)  83.3 us
    dot_general x8, matrix products, product(): jnp.dot(masked_a(panel_a, mask_a), masked_b(panel_b, mask_b), preferred_e...  56.9 us
    ppermute x40, starting transfers between devices, from_behind(): return lax.ppermute(value, axis, pairs)  54.5 us
    ppermute x7, waiting for transfers between devices, on_device(): part = lax.ppermute(part, 'row', [(d, d ^ mask_2) for d in range(ways)])  43.1 us
    convert_element_type x1, other arithmetic, on_device(): result = total.astype(jnp.bfloat16)  9.3 us
    ppermute x7, starting transfers between devices, on_device(): part = lax.ppermute(part, 'row', [(d, d ^ mask_2) for d in range(ways)])  5.94 us
  transfers between devices with their start and end apart: 47, of which 10 were waited for; matrix products, arithmetic and copies ran while one was open for 21% of the time, Pallas kernels for 0%

profile of v1, /device:TPU:0, one launch (start us, length us, event | category | flops | bytes accessed | tf_op | source)
XLA Modules:
  0.0 282.4 jit_solution(15024980332956054278)
XLA Ops:
  0.0 5.0 %collective-permute-start.4 = (bf16[2048,256]{1,0:T(8,128)(2,1)}, bf16[2048,256]{1,0:T(8,128)(2,1)S(1)}, u32[]{:S(2)}, u32[]{:S(2)}) collective-permute-start(bf16[2048,256]{1,0:T(8,128)(2,1)} %param.7), channel_id=1, source_target_pairs={{0,3},{1,0},{2,1},{3,2},{4,7},{5,4},{6,5},{7,6},{8,11},{9,8},{10,9... | collective-permute-start | bytes 3145736 | tf_op jit(solution)/shard_map/ppermute | solution.py:12
  5.5 1.3 collective-permute-start.10
  6.8 1.2 collective-permute-start.13
  9.0 18.8 %collective-permute-done.4 = bf16[2048,256]{1,0:T(8,128)(2,1)S(1)} collective-permute-done((bf16[2048,256]{1,0:T(8,128)(2,1)}, bf16[2048,256]{1,0:T(8,128)(2,1)S(1)}, u32[]{:S(2)}, u32[]{:S(2)}) %collective-permute-start.4) | collective-permute-done | bytes 1048608 | tf_op jit(solution)/shard_map/ppermute | solution.py:12
  27.8 1.3 broadcast_select_fusion
  29.1 1.4 collective-permute-start.5
  31.9 1.2 collective-permute-start.14
  33.1 2.3 collective-permute-done.14
  35.4 1.5 collective-permute-start.15
  37.6 1.6 collective-permute-start.8
  40.7 35.9 %collective-permute-done.5 = bf16[2048,256]{1,0:T(8,128)(2,1)S(1)} collective-permute-done((bf16[2048,256]{1,0:T(8,128)(2,1)S(1)}, bf16[2048,256]{1,0:T(8,128)(2,1)S(1)}, u32[]{:S(2)}, u32[]{:S(2)}) %collective-permute-start.5) | collective-permute-done | bytes 1048608 | tf_op jit(solution)/shard_map/ppermute | solution.py:12
  76.7 2.3 collective-permute-start.6
  79.2 1.6 collective-permute-start.12
  80.8 20.9 %collective-permute-done.9 = s32[16,2]{0,1:T(2,128)S(1)} collective-permute-done((s32[16,2]{0,1:T(2,128)S(1)}, s32[16,2]{0,1:T(2,128)S(1)}, u32[]{:S(2)}, u32[]{:S(2)}) %collective-permute-start.9) | collective-permute-done | bytes 160 | tf_op jit(solution)/shard_map/ppermute | solution.py:12
  102.2 97.0 %while.19 = (s32[]{:T(128)}, f32[2048,1024]{1,0:T(8,128)}, bf16[2048,256]{1,0:T(8,128)(2,1)S(1)}, s32[16,2]{0,1:T(2,128)S(1)}, bf16[128,1024]{1,0:T(8,128)(2,1)S...) while((s32[]{:T(128)}, f32[2048,1024]{1,0:T(8,128)}, bf16[2048,256]{1,0:T(8,128)(2,1)S(1)}, ...), condition=%wide.region_2.3_spmd.clone, body=%wide.region_1.2_spmd.clone.sunk | while | flops 543555584 | bytes 25441596 | solution.py:73
  102.2 4.4 %collective-permute-start = (bf16[2048,128]{1,0:T(8,128)(2,1)S(1)}, bf16[2048,128]{1,0:T(8,128)(2,1)S(1)}, u32[]{:S(2)}, u32[]{:S(2)}) collective-permute-start(bf16[2048,128]{1,0:T(8,128)(2,1)S(1)} %get-tuple-element.135), channel_id=1, source_target_pairs={{0,3},{1,0},{2,1},{3,2},{4,7},{5,4},{6,5},{7,6},{8,11},{9,8},{10,9... | collective-permute-start | bytes 1572872 | tf_op jit(solution)/shard_map/while/body/eval_jaxpr/ppermute | solution.py:12
  106.8 1.3 collective-permute-start.3
  108.2 4.6 %select_add_fusion.2 = f32[2048,1024]{1,0:T(8,128)} fusion(f32[2048,1024]{1,0:T(8,128)} %get-tuple-element.148, pred[]{:T(512)S(6)} %compare.6, bf16[128,1024]{1,0:T(8,128)(2,1)S(1)} %copy.16, bf16[2048]{0:T(1024)(128)(2,1)S(1)} %broadcast_bitcast_fusion.6, bf16[1024]{0:T(1024)(128)(2,1)S(1)} %broadcast_bitcast_fusion.7, ...), kind=kOutput, calls=%fused_computation.clone.1 | convolution fusion | flops 541458432 | bytes 17569792 | tf_op jit(solution)/shard_map/while/body/eval_jaxpr/dot_general | solution.py:30
  112.8 4.3 %collective-permute-done.1 = s32[16,1]{0,1:T(1,128)S(1)} collective-permute-done((s32[16,1]{0,1:T(1,128)S(1)}, s32[16,1]{0,1:T(1,128)S(1)}, u32[]{:S(2)}, u32[]{:S(2)}) %collective-permute-start.1) | collective-permute-done | bytes 96 | tf_op jit(solution)/shard_map/while/body/eval_jaxpr/ppermute | solution.py:12
  117.4 4.4 %collective-permute-start = (bf16[2048,128]{1,0:T(8,128)(2,1)S(1)}, bf16[2048,128]{1,0:T(8,128)(2,1)S(1)}, u32[]{:S(2)}, u32[]{:S(2)}) collective-permute-start(bf16[2048,128]{1,0:T(8,128)(2,1)S(1)} %get-tuple-element.135), channel_id=1, source_target_pairs={{0,3},{1,0},{2,1},{3,2},{4,7},{5,4},{6,5},{7,6},{8,11},{9,8},{10,9... | collective-permute-start | bytes 1572872 | tf_op jit(solution)/shard_map/while/body/eval_jaxpr/ppermute | solution.py:12
  121.9 1.3 collective-permute-start.3
  123.3 8.0 %select_add_fusion.2 = f32[2048,1024]{1,0:T(8,128)} fusion(f32[2048,1024]{1,0:T(8,128)} %get-tuple-element.148, pred[]{:T(512)S(6)} %compare.6, bf16[128,1024]{1,0:T(8,128)(2,1)S(1)} %copy.16, bf16[2048]{0:T(1024)(128)(2,1)S(1)} %broadcast_bitcast_fusion.6, bf16[1024]{0:T(1024)(128)(2,1)S(1)} %broadcast_bitcast_fusion.7, ...), kind=kOutput, calls=%fused_computation.clone.1 | convolution fusion | flops 541458432 | bytes 17569792 | tf_op jit(solution)/shard_map/while/body/eval_jaxpr/dot_general | solution.py:30
  131.6 4.2 %collective-permute-start = (bf16[2048,128]{1,0:T(8,128)(2,1)S(1)}, bf16[2048,128]{1,0:T(8,128)(2,1)S(1)}, u32[]{:S(2)}, u32[]{:S(2)}) collective-permute-start(bf16[2048,128]{1,0:T(8,128)(2,1)S(1)} %get-tuple-element.135), channel_id=1, source_target_pairs={{0,3},{1,0},{2,1},{3,2},{4,7},{5,4},{6,5},{7,6},{8,11},{9,8},{10,9... | collective-permute-start | bytes 1572872 | tf_op jit(solution)/shard_map/while/body/eval_jaxpr/ppermute | solution.py:12
  136.0 1.3 collective-permute-start.3
  137.5 8.0 %select_add_fusion.2 = f32[2048,1024]{1,0:T(8,128)} fusion(f32[2048,1024]{1,0:T(8,128)} %get-tuple-element.148, pred[]{:T(512)S(6)} %compare.6, bf16[128,1024]{1,0:T(8,128)(2,1)S(1)} %copy.16, bf16[2048]{0:T(1024)(128)(2,1)S(1)} %broadcast_bitcast_fusion.6, bf16[1024]{0:T(1024)(128)(2,1)S(1)} %broadcast_bitcast_fusion.7, ...), kind=kOutput, calls=%fused_computation.clone.1 | convolution fusion | flops 541458432 | bytes 17569792 | tf_op jit(solution)/shard_map/while/body/eval_jaxpr/dot_general | solution.py:30
  145.7 3.3 %collective-permute-start = (bf16[2048,128]{1,0:T(8,128)(2,1)S(1)}, bf16[2048,128]{1,0:T(8,128)(2,1)S(1)}, u32[]{:S(2)}, u32[]{:S(2)}) collective-permute-start(bf16[2048,128]{1,0:T(8,128)(2,1)S(1)} %get-tuple-element.135), channel_id=1, source_target_pairs={{0,3},{1,0},{2,1},{3,2},{4,7},{5,4},{6,5},{7,6},{8,11},{9,8},{10,9... | collective-permute-start | bytes 1572872 | tf_op jit(solution)/shard_map/while/body/eval_jaxpr/ppermute | solution.py:12
  149.1 1.3 collective-permute-start.3
  150.6 8.0 %select_add_fusion.2 = f32[2048,1024]{1,0:T(8,128)} fusion(f32[2048,1024]{1,0:T(8,128)} %get-tuple-element.148, pred[]{:T(512)S(6)} %compare.6, bf16[128,1024]{1,0:T(8,128)(2,1)S(1)} %copy.16, bf16[2048]{0:T(1024)(128)(2,1)S(1)} %broadcast_bitcast_fusion.6, bf16[1024]{0:T(1024)(128)(2,1)S(1)} %broadcast_bitcast_fusion.7, ...), kind=kOutput, calls=%fused_computation.clone.1 | convolution fusion | flops 541458432 | bytes 17569792 | tf_op jit(solution)/shard_map/while/body/eval_jaxpr/dot_general | solution.py:30
  159.4 2.2 collective-permute-start
  161.8 1.8 collective-permute-start.3
  163.8 8.0 %select_add_fusion.2 = f32[2048,1024]{1,0:T(8,128)} fusion(f32[2048,1024]{1,0:T(8,128)} %get-tuple-element.148, pred[]{:T(512)S(6)} %compare.6, bf16[128,1024]{1,0:T(8,128)(2,1)S(1)} %copy.16, bf16[2048]{0:T(1024)(128)(2,1)S(1)} %broadcast_bitcast_fusion.6, bf16[1024]{0:T(1024)(128)(2,1)S(1)} %broadcast_bitcast_fusion.7, ...), kind=kOutput, calls=%fused_computation.clone.1 | convolution fusion | flops 541458432 | bytes 17569792 | tf_op jit(solution)/shard_map/while/body/eval_jaxpr/dot_general | solution.py:30
  172.5 3.2 %collective-permute-start = (bf16[2048,128]{1,0:T(8,128)(2,1)S(1)}, bf16[2048,128]{1,0:T(8,128)(2,1)S(1)}, u32[]{:S(2)}, u32[]{:S(2)}) collective-permute-start(bf16[2048,128]{1,0:T(8,128)(2,1)S(1)} %get-tuple-element.135), channel_id=1, source_target_pairs={{0,3},{1,0},{2,1},{3,2},{4,7},{5,4},{6,5},{7,6},{8,11},{9,8},{10,9... | collective-permute-start | bytes 1572872 | tf_op jit(solution)/shard_map/while/body/eval_jaxpr/ppermute | solution.py:12
  175.9 1.9 collective-permute-start.3
  177.9 8.0 %select_add_fusion.2 = f32[2048,1024]{1,0:T(8,128)} fusion(f32[2048,1024]{1,0:T(8,128)} %get-tuple-element.148, pred[]{:T(512)S(6)} %compare.6, bf16[128,1024]{1,0:T(8,128)(2,1)S(1)} %copy.16, bf16[2048]{0:T(1024)(128)(2,1)S(1)} %broadcast_bitcast_fusion.6, bf16[1024]{0:T(1024)(128)(2,1)S(1)} %broadcast_bitcast_fusion.7, ...), kind=kOutput, calls=%fused_computation.clone.1 | convolution fusion | flops 541458432 | bytes 17569792 | tf_op jit(solution)/shard_map/while/body/eval_jaxpr/dot_general | solution.py:30
  186.1 3.0 %collective-permute-start = (bf16[2048,128]{1,0:T(8,128)(2,1)S(1)}, bf16[2048,128]{1,0:T(8,128)(2,1)S(1)}, u32[]{:S(2)}, u32[]{:S(2)}) collective-permute-start(bf16[2048,128]{1,0:T(8,128)(2,1)S(1)} %get-tuple-element.135), channel_id=1, source_target_pairs={{0,3},{1,0},{2,1},{3,2},{4,7},{5,4},{6,5},{7,6},{8,11},{9,8},{10,9... | collective-permute-start | bytes 1572872 | tf_op jit(solution)/shard_map/while/body/eval_jaxpr/ppermute | solution.py:12
  189.3 1.5 collective-permute-start.3
  191.0 8.0 %select_add_fusion.2 = f32[2048,1024]{1,0:T(8,128)} fusion(f32[2048,1024]{1,0:T(8,128)} %get-tuple-element.148, pred[]{:T(512)S(6)} %compare.6, bf16[128,1024]{1,0:T(8,128)(2,1)S(1)} %copy.16, bf16[2048]{0:T(1024)(128)(2,1)S(1)} %broadcast_bitcast_fusion.6, bf16[1024]{0:T(1024)(128)(2,1)S(1)} %broadcast_bitcast_fusion.7, ...), kind=kOutput, calls=%fused_computation.clone.1 | convolution fusion | flops 541458432 | bytes 17569792 | tf_op jit(solution)/shard_map/while/body/eval_jaxpr/dot_general | solution.py:30
  199.3 4.5 %fusion.6 = f32[2048,1024]{1,0:T(8,128)} fusion(bf16[2048,256]{1,0:T(8,128)(2,1)S(1)} %get-tuple-element.42, bf16[128,1024]{1,0:T(8,128)(2,1)S(1)} %get-tuple-element.44, bf16[2048]{0:T(1024)(128)(2,1)S(1)} %broadcast_bitcast_fusion.2, bf16[1024]{0:T(1024)(128)(2,1)S(1)} %broadcast_bitcast_fusion.3), kind=kOutput, calls=%fused_computation.20 | convolution fusion | flops 537264128 | bytes 9181184 | tf_op jit(solution)/shard_map/dot_general | solution.py:30
  203.9 9.3 %add_convert_fusion = bf16[2048,1024]{1,0:T(8,128)(2,1)} fusion(f32[2048,1024]{1,0:T(8,128)} %get-tuple-element.41, f32[2048,1024]{1,0:T(8,128)} %fusion.6), kind=kLoop, calls=%fused_computation.13 | loop fusion | flops 4194304 | bytes 20971520 | tf_op jit(solution)/shard_map/convert_element_type | solution.py:77
  213.2 4.8 %reshape.54 = bf16[16,131072]{1,0:T(8,128)(2,1)} reshape(bf16[2048,1024]{1,0:T(8,128)(2,1)} %add_convert_fusion) | data formatting | bytes 8388608 | tf_op jit(solution)/shard_map/reshape | solution.py:91
  218.0 5.4 %convolution_convert_fusion = bf16[16,131072]{1,0:T(8,128)(2,1)} fusion(bf16[16,131072]{1,0:T(8,128)(2,1)} %reshape.54, s32[16]{0:T(128)S(1)} %multiply_add_fusion), kind=kOutput, calls=%fused_computation.12 | convolution fusion | flops 69206272 | bytes 8388672 | tf_op jit(solution)/shard_map/dot_general | solution.py:90
  223.4 4.8 %reshape.55 = bf16[8,256,1024]{2,1,0:T(8,128)(2,1)} reshape(bf16[16,131072]{1,0:T(8,128)(2,1)} %convolution_convert_fusion) | data formatting | bytes 8388608 | tf_op jit(solution)/shard_map/reshape | solution.py:93
  228.7 1.7 copy-done
  234.6 1.7 collective-permute-start.21
  236.4 9.4 %collective-permute-done.17 = bf16[1,256,1024]{2,1,0:T(8,128)(2,1)S(1)} collective-permute-done((bf16[1,256,1024]{2,1,0:T(8,128)(2,1)S(1)}, bf16[1,256,1024]{2,1,0:T(8,128)(2,1)S(1)}, u32[]{:S(2)}, u32[]{:S(2)}) %collective-permute-start.17) | collective-permute-done | bytes 524320 | tf_op jit(solution)/shard_map/ppermute | solution.py:104
  246.5 9.7 %collective-permute-done.18 = bf16[1,256,1024]{2,1,0:T(8,128)(2,1)S(1)} collective-permute-done((bf16[1,256,1024]{2,1,0:T(8,128)(2,1)S(1)}, bf16[1,256,1024]{2,1,0:T(8,128)(2,1)S(1)}, u32[]{:S(2)}, u32[]{:S(2)}) %collective-permute-start.18) | collective-permute-done | bytes 524320 | tf_op jit(solution)/shard_map/ppermute | solution.py:104
  256.3 23.9 %collective-permute-done.20 = bf16[1,256,1024]{2,1,0:T(8,128)(2,1)S(1)} collective-permute-done((bf16[1,256,1024]{2,1,0:T(8,128)(2,1)S(1)}, bf16[1,256,1024]{2,1,0:T(8,128)(2,1)S(1)}, u32[]{:S(2)}, u32[]{:S(2)}) %collective-permute-start.20) | collective-permute-done | bytes 524320 | tf_op jit(solution)/shard_map/ppermute | solution.py:104
  280.4 2.0 copy-done.1
  (156 shorter events, 15.9 us)
Async XLA Ops:
  0.0 27.8 %collective-permute-start.4 = (bf16[2048,256]{1,0:T(8,128)(2,1)}, bf16[2048,256]{1,0:T(8,128)(2,1)S(1)}, u32[]{:S(2)}, u32[]{:S(2)}) collective-permute-start(bf16[2048,256]{1,0:T(8,128)(2,1)} %param.7), channel_id=1, source_target_pairs={{0,3},{1,0},{2,1},{3,2},{4,7},{5,4},{6,5},{7,6},{8,11},{9,8},{10,9... | collective-permute-start | bytes 3145736 | tf_op jit(solution)/shard_map/ppermute | solution.py:12
  5.0 31.9 %collective-permute-start.7 = (s32[16,2]{0,1:T(2,128)}, s32[16,2]{0,1:T(2,128)S(1)}, u32[]{:S(2)}, u32[]{:S(2)}) collective-permute-start(s32[16,2]{0,1:T(2,128)} %param.8), channel_id=1, source_target_pairs={{0,3},{1,0},{2,1},{3,2},{4,7},{5,4},{6,5},{7,6},{8,11},{9,8},{10,9... | collective-permute-start | bytes 392 | tf_op jit(solution)/shard_map/ppermute | solution.py:12
  5.5 33.7 %collective-permute-start.10 = (bf16[128,1024]{1,0:T(8,128)(2,1)}, bf16[128,1024]{1,0:T(8,128)(2,1)S(1)}, u32[]{:S(2)}, u32[]{:S(2)}) collective-permute-start(bf16[128,1024]{1,0:T(8,128)(2,1)} %param.9), channel_id=1, source_target_pairs={{0,28},{4,0},{8,4},{12,8},{16,12},{20,16},{24,20},{28,24},{1,29},{... | collective-permute-start | bytes 786440 | tf_op jit(solution)/shard_map/ppermute | solution.py:12
  6.8 24.4 %collective-permute-start.13 = (s32[1,8]{1,0:T(1,128)}, s32[1,8]{1,0:T(1,128)S(1)}, u32[]{:S(2)}, u32[]{:S(2)}) collective-permute-start(s32[1,8]{1,0:T(1,128)} %param.10), channel_id=1, source_target_pairs={{0,28},{4,0},{8,4},{12,8},{16,12},{20,16},{24,20},{28,24},{1,29},{... | collective-permute-start | bytes 104 | tf_op jit(solution)/shard_map/ppermute | solution.py:12
  29.1 47.5 %collective-permute-start.5 = (bf16[2048,256]{1,0:T(8,128)(2,1)S(1)}, bf16[2048,256]{1,0:T(8,128)(2,1)S(1)}, u32[]{:S(2)}, u32[]{:S(2)}) collective-permute-start(bf16[2048,256]{1,0:T(8,128)(2,1)S(1)} %broadcast_select_fusion), channel_id=1, source_target_pairs={{0,2},{1,3},{2,0},{3,1},{4,6},{5,7},{6,4},{7,5},{8,10},{9,11},{10,... | collective-permute-start | bytes 3145736 | tf_op jit(solution)/shard_map/ppermute | solution.py:12
  31.9 3.5 %collective-permute-start.14 = (s32[1,8]{1,0:T(1,128)S(1)}, s32[1,8]{1,0:T(1,128)S(1)}, u32[]{:S(2)}, u32[]{:S(2)}) collective-permute-start(s32[1,8]{1,0:T(1,128)S(1)} %broadcast_select_fusion.5), channel_id=1, source_target_pairs={{0,24},{4,28},{8,0},{12,4},{16,8},{20,12},{24,16},{28,20},{1,25},{... | collective-permute-start | bytes 104 | tf_op jit(solution)/shard_map/ppermute | solution.py:12
  35.4 45.3 %collective-permute-start.15 = (s32[1,8]{1,0:T(1,128)S(1)}, s32[1,8]{1,0:T(1,128)S(1)}, u32[]{:S(2)}, u32[]{:S(2)}) collective-permute-start(s32[1,8]{1,0:T(1,128)S(1)} %broadcast_select_fusion.6), channel_id=1, source_target_pairs={{0,16},{4,20},{8,24},{12,28},{16,0},{20,4},{24,8},{28,12},{1,17},{... | collective-permute-start | bytes 104 | tf_op jit(solution)/shard_map/ppermute | solution.py:12
  37.6 41.4 %collective-permute-start.8 = (s32[16,2]{0,1:T(2,128)S(1)}, s32[16,2]{0,1:T(2,128)S(1)}, u32[]{:S(2)}, u32[]{:S(2)}) collective-permute-start(s32[16,2]{0,1:T(2,128)S(1)} %broadcast_select_fusion.8), channel_id=1, source_target_pairs={{0,2},{1,3},{2,0},{3,1},{4,6},{5,7},{6,4},{7,5},{8,10},{9,11},{10,... | collective-permute-start | bytes 392 | tf_op jit(solution)/shard_map/ppermute | solution.py:12
  40.2 39.0 %collective-permute-start.11 = (bf16[128,1024]{1,0:T(8,128)(2,1)S(1)}, bf16[128,1024]{1,0:T(8,128)(2,1)S(1)}, u32[]{:S(2)}, u32[]{:S(2)}) collective-permute-start(bf16[128,1024]{1,0:T(8,128)(2,1)S(1)} %broadcast_select_fusion.2), channel_id=1, source_target_pairs={{0,24},{4,28},{8,0},{12,4},{16,8},{20,12},{24,16},{28,20},{1,25},{... | collective-permute-start | bytes 786440 | tf_op jit(solution)/shard_map/ppermute | solution.py:12
  76.7 25.0 %collective-permute-start.6 = (bf16[2048,256]{1,0:T(8,128)(2,1)S(1)}, bf16[2048,256]{1,0:T(8,128)(2,1)S(1)}, u32[]{:S(2)}, u32[]{:S(2)}) collective-permute-start(bf16[2048,256]{1,0:T(8,128)(2,1)S(1)} %broadcast_select_fusion.1), channel_id=1, source_target_pairs={{0,3},{1,0},{2,1},{3,2},{4,7},{5,4},{6,5},{7,6},{8,11},{9,8},{10,9... | collective-permute-start | bytes 3145736 | tf_op jit(solution)/shard_map/ppermute | solution.py:12
  79.1 22.6 %collective-permute-start.9 = (s32[16,2]{0,1:T(2,128)S(1)}, s32[16,2]{0,1:T(2,128)S(1)}, u32[]{:S(2)}, u32[]{:S(2)}) collective-permute-start(s32[16,2]{0,1:T(2,128)S(1)} %broadcast_select_fusion.9), channel_id=1, source_target_pairs={{0,3},{1,0},{2,1},{3,2},{4,7},{5,4},{6,5},{7,6},{8,11},{9,8},{10,9... | collective-permute-start | bytes 392 | tf_op jit(solution)/shard_map/ppermute | solution.py:12
  79.2 22.5 %collective-permute-start.12 = (bf16[128,1024]{1,0:T(8,128)(2,1)S(1)}, bf16[128,1024]{1,0:T(8,128)(2,1)S(1)}, u32[]{:S(2)}, u32[]{:S(2)}) collective-permute-start(bf16[128,1024]{1,0:T(8,128)(2,1)S(1)} %broadcast_select_fusion.3), channel_id=1, source_target_pairs={{0,16},{4,20},{8,24},{12,28},{16,0},{20,4},{24,8},{28,12},{1,17},{... | collective-permute-start | bytes 786440 | tf_op jit(solution)/shard_map/ppermute | solution.py:12
  102.2 14.9 %collective-permute-start = (bf16[2048,128]{1,0:T(8,128)(2,1)S(1)}, bf16[2048,128]{1,0:T(8,128)(2,1)S(1)}, u32[]{:S(2)}, u32[]{:S(2)}) collective-permute-start(bf16[2048,128]{1,0:T(8,128)(2,1)S(1)} %get-tuple-element.135), channel_id=1, source_target_pairs={{0,3},{1,0},{2,1},{3,2},{4,7},{5,4},{6,5},{7,6},{8,11},{9,8},{10,9... | collective-permute-start | bytes 1572872 | tf_op jit(solution)/shard_map/while/body/eval_jaxpr/ppermute | solution.py:12
  106.6 10.5 %collective-permute-start.1 = (s32[16,1]{0,1:T(1,128)S(1)}, s32[16,1]{0,1:T(1,128)S(1)}, u32[]{:S(2)}, u32[]{:S(2)}) collective-permute-start(s32[16,1]{0,1:T(1,128)S(1)} %get-tuple-element.137), channel_id=1, source_target_pairs={{0,3},{1,0},{2,1},{3,2},{4,7},{5,4},{6,5},{7,6},{8,11},{9,8},{10,9... | collective-permute-start | bytes 200 | tf_op jit(solution)/shard_map/while/body/eval_jaxpr/ppermute | solution.py:12
  106.7 10.6 %collective-permute-start.2 = (bf16[128,1024]{1,0:T(8,128)(2,1)S(1)}, bf16[128,1024]{1,0:T(8,128)(2,1)S(1)}, u32[]{:S(2)}, u32[]{:S(2)}) collective-permute-start(bf16[128,1024]{1,0:T(8,128)(2,1)S(1)} %copy.16), channel_id=1, source_target_pairs={{0,28},{4,0},{8,4},{12,8},{16,12},{20,16},{24,20},{28,24},{1,29},{... | collective-permute-start | bytes 786440 | tf_op jit(solution)/shard_map/while/body/eval_jaxpr/ppermute | solution.py:12
  106.8 10.5 %collective-permute-start.3 = (s32[1,8]{1,0:T(1,128)S(1)}, s32[1,8]{1,0:T(1,128)S(1)}, u32[]{:S(2)}, u32[]{:S(2)}) collective-permute-start(s32[1,8]{1,0:T(1,128)S(1)} %copy.17), channel_id=1, source_target_pairs={{0,28},{4,0},{8,4},{12,8},{16,12},{20,16},{24,20},{28,24},{1,29},{... | collective-permute-start | bytes 104 | tf_op jit(solution)/shard_map/while/body/eval_jaxpr/ppermute | solution.py:12
  117.4 14.0 %collective-permute-start = (bf16[2048,128]{1,0:T(8,128)(2,1)S(1)}, bf16[2048,128]{1,0:T(8,128)(2,1)S(1)}, u32[]{:S(2)}, u32[]{:S(2)}) collective-permute-start(bf16[2048,128]{1,0:T(8,128)(2,1)S(1)} %get-tuple-element.135), channel_id=1, source_target_pairs={{0,3},{1,0},{2,1},{3,2},{4,7},{5,4},{6,5},{7,6},{8,11},{9,8},{10,9... | collective-permute-start | bytes 1572872 | tf_op jit(solution)/shard_map/while/body/eval_jaxpr/ppermute | solution.py:12
  121.7 9.6 %collective-permute-start.1 = (s32[16,1]{0,1:T(1,128)S(1)}, s32[16,1]{0,1:T(1,128)S(1)}, u32[]{:S(2)}, u32[]{:S(2)}) collective-permute-start(s32[16,1]{0,1:T(1,128)S(1)} %get-tuple-element.137), channel_id=1, source_target_pairs={{0,3},{1,0},{2,1},{3,2},{4,7},{5,4},{6,5},{7,6},{8,11},{9,8},{10,9... | collective-permute-start | bytes 200 | tf_op jit(solution)/shard_map/while/body/eval_jaxpr/ppermute | solution.py:12
  121.8 9.7 %collective-permute-start.2 = (bf16[128,1024]{1,0:T(8,128)(2,1)S(1)}, bf16[128,1024]{1,0:T(8,128)(2,1)S(1)}, u32[]{:S(2)}, u32[]{:S(2)}) collective-permute-start(bf16[128,1024]{1,0:T(8,128)(2,1)S(1)} %copy.16), channel_id=1, source_target_pairs={{0,28},{4,0},{8,4},{12,8},{16,12},{20,16},{24,20},{28,24},{1,29},{... | collective-permute-start | bytes 786440 | tf_op jit(solution)/shard_map/while/body/eval_jaxpr/ppermute | solution.py:12
  121.9 9.6 %collective-permute-start.3 = (s32[1,8]{1,0:T(1,128)S(1)}, s32[1,8]{1,0:T(1,128)S(1)}, u32[]{:S(2)}, u32[]{:S(2)}) collective-permute-start(s32[1,8]{1,0:T(1,128)S(1)} %copy.17), channel_id=1, source_target_pairs={{0,28},{4,0},{8,4},{12,8},{16,12},{20,16},{24,20},{28,24},{1,29},{... | collective-permute-start | bytes 104 | tf_op jit(solution)/shard_map/while/body/eval_jaxpr/ppermute | solution.py:12
  131.6 13.9 %collective-permute-start = (bf16[2048,128]{1,0:T(8,128)(2,1)S(1)}, bf16[2048,128]{1,0:T(8,128)(2,1)S(1)}, u32[]{:S(2)}, u32[]{:S(2)}) collective-permute-start(bf16[2048,128]{1,0:T(8,128)(2,1)S(1)} %get-tuple-element.135), channel_id=1, source_target_pairs={{0,3},{1,0},{2,1},{3,2},{4,7},{5,4},{6,5},{7,6},{8,11},{9,8},{10,9... | collective-permute-start | bytes 1572872 | tf_op jit(solution)/shard_map/while/body/eval_jaxpr/ppermute | solution.py:12
  135.8 9.6 %collective-permute-start.1 = (s32[16,1]{0,1:T(1,128)S(1)}, s32[16,1]{0,1:T(1,128)S(1)}, u32[]{:S(2)}, u32[]{:S(2)}) collective-permute-start(s32[16,1]{0,1:T(1,128)S(1)} %get-tuple-element.137), channel_id=1, source_target_pairs={{0,3},{1,0},{2,1},{3,2},{4,7},{5,4},{6,5},{7,6},{8,11},{9,8},{10,9... | collective-permute-start | bytes 200 | tf_op jit(solution)/shard_map/while/body/eval_jaxpr/ppermute | solution.py:12
  135.9 9.7 %collective-permute-start.2 = (bf16[128,1024]{1,0:T(8,128)(2,1)S(1)}, bf16[128,1024]{1,0:T(8,128)(2,1)S(1)}, u32[]{:S(2)}, u32[]{:S(2)}) collective-permute-start(bf16[128,1024]{1,0:T(8,128)(2,1)S(1)} %copy.16), channel_id=1, source_target_pairs={{0,28},{4,0},{8,4},{12,8},{16,12},{20,16},{24,20},{28,24},{1,29},{... | collective-permute-start | bytes 786440 | tf_op jit(solution)/shard_map/while/body/eval_jaxpr/ppermute | solution.py:12
  136.0 9.6 %collective-permute-start.3 = (s32[1,8]{1,0:T(1,128)S(1)}, s32[1,8]{1,0:T(1,128)S(1)}, u32[]{:S(2)}, u32[]{:S(2)}) collective-permute-start(s32[1,8]{1,0:T(1,128)S(1)} %copy.17), channel_id=1, source_target_pairs={{0,28},{4,0},{8,4},{12,8},{16,12},{20,16},{24,20},{28,24},{1,29},{... | collective-permute-start | bytes 104 | tf_op jit(solution)/shard_map/while/body/eval_jaxpr/ppermute | solution.py:12
  145.7 13.4 %collective-permute-start = (bf16[2048,128]{1,0:T(8,128)(2,1)S(1)}, bf16[2048,128]{1,0:T(8,128)(2,1)S(1)}, u32[]{:S(2)}, u32[]{:S(2)}) collective-permute-start(bf16[2048,128]{1,0:T(8,128)(2,1)S(1)} %get-tuple-element.135), channel_id=1, source_target_pairs={{0,3},{1,0},{2,1},{3,2},{4,7},{5,4},{6,5},{7,6},{8,11},{9,8},{10,9... | collective-permute-start | bytes 1572872 | tf_op jit(solution)/shard_map/while/body/eval_jaxpr/ppermute | solution.py:12
  149.0 10.1 %collective-permute-start.1 = (s32[16,1]{0,1:T(1,128)S(1)}, s32[16,1]{0,1:T(1,128)S(1)}, u32[]{:S(2)}, u32[]{:S(2)}) collective-permute-start(s32[16,1]{0,1:T(1,128)S(1)} %get-tuple-element.137), channel_id=1, source_target_pairs={{0,3},{1,0},{2,1},{3,2},{4,7},{5,4},{6,5},{7,6},{8,11},{9,8},{10,9... | collective-permute-start | bytes 200 | tf_op jit(solution)/shard_map/while/body/eval_jaxpr/ppermute | solution.py:12
  149.1 10.2 %collective-permute-start.2 = (bf16[128,1024]{1,0:T(8,128)(2,1)S(1)}, bf16[128,1024]{1,0:T(8,128)(2,1)S(1)}, u32[]{:S(2)}, u32[]{:S(2)}) collective-permute-start(bf16[128,1024]{1,0:T(8,128)(2,1)S(1)} %copy.16), channel_id=1, source_target_pairs={{0,28},{4,0},{8,4},{12,8},{16,12},{20,16},{24,20},{28,24},{1,29},{... | collective-permute-start | bytes 786440 | tf_op jit(solution)/shard_map/while/body/eval_jaxpr/ppermute | solution.py:12
  149.1 10.1 %collective-permute-start.3 = (s32[1,8]{1,0:T(1,128)S(1)}, s32[1,8]{1,0:T(1,128)S(1)}, u32[]{:S(2)}, u32[]{:S(2)}) collective-permute-start(s32[1,8]{1,0:T(1,128)S(1)} %copy.17), channel_id=1, source_target_pairs={{0,28},{4,0},{8,4},{12,8},{16,12},{20,16},{24,20},{28,24},{1,29},{... | collective-permute-start | bytes 104 | tf_op jit(solution)/shard_map/while/body/eval_jaxpr/ppermute | solution.py:12
  159.4 12.9 %collective-permute-start = (bf16[2048,128]{1,0:T(8,128)(2,1)S(1)}, bf16[2048,128]{1,0:T(8,128)(2,1)S(1)}, u32[]{:S(2)}, u32[]{:S(2)}) collective-permute-start(bf16[2048,128]{1,0:T(8,128)(2,1)S(1)} %get-tuple-element.135), channel_id=1, source_target_pairs={{0,3},{1,0},{2,1},{3,2},{4,7},{5,4},{6,5},{7,6},{8,11},{9,8},{10,9... | collective-permute-start | bytes 1572872 | tf_op jit(solution)/shard_map/while/body/eval_jaxpr/ppermute | solution.py:12
  161.6 10.6 %collective-permute-start.1 = (s32[16,1]{0,1:T(1,128)S(1)}, s32[16,1]{0,1:T(1,128)S(1)}, u32[]{:S(2)}, u32[]{:S(2)}) collective-permute-start(s32[16,1]{0,1:T(1,128)S(1)} %get-tuple-element.137), channel_id=1, source_target_pairs={{0,3},{1,0},{2,1},{3,2},{4,7},{5,4},{6,5},{7,6},{8,11},{9,8},{10,9... | collective-permute-start | bytes 200 | tf_op jit(solution)/shard_map/while/body/eval_jaxpr/ppermute | solution.py:12
  161.7 10.7 %collective-permute-start.2 = (bf16[128,1024]{1,0:T(8,128)(2,1)S(1)}, bf16[128,1024]{1,0:T(8,128)(2,1)S(1)}, u32[]{:S(2)}, u32[]{:S(2)}) collective-permute-start(bf16[128,1024]{1,0:T(8,128)(2,1)S(1)} %copy.16), channel_id=1, source_target_pairs={{0,28},{4,0},{8,4},{12,8},{16,12},{20,16},{24,20},{28,24},{1,29},{... | collective-permute-start | bytes 786440 | tf_op jit(solution)/shard_map/while/body/eval_jaxpr/ppermute | solution.py:12
  161.8 10.6 %collective-permute-start.3 = (s32[1,8]{1,0:T(1,128)S(1)}, s32[1,8]{1,0:T(1,128)S(1)}, u32[]{:S(2)}, u32[]{:S(2)}) collective-permute-start(s32[1,8]{1,0:T(1,128)S(1)} %copy.17), channel_id=1, source_target_pairs={{0,28},{4,0},{8,4},{12,8},{16,12},{20,16},{24,20},{28,24},{1,29},{... | collective-permute-start | bytes 104 | tf_op jit(solution)/shard_map/while/body/eval_jaxpr/ppermute | solution.py:12
  172.5 13.4 %collective-permute-start = (bf16[2048,128]{1,0:T(8,128)(2,1)S(1)}, bf16[2048,128]{1,0:T(8,128)(2,1)S(1)}, u32[]{:S(2)}, u32[]{:S(2)}) collective-permute-start(bf16[2048,128]{1,0:T(8,128)(2,1)S(1)} %get-tuple-element.135), channel_id=1, source_target_pairs={{0,3},{1,0},{2,1},{3,2},{4,7},{5,4},{6,5},{7,6},{8,11},{9,8},{10,9... | collective-permute-start | bytes 1572872 | tf_op jit(solution)/shard_map/while/body/eval_jaxpr/ppermute | solution.py:12
  175.7 10.1 %collective-permute-start.1 = (s32[16,1]{0,1:T(1,128)S(1)}, s32[16,1]{0,1:T(1,128)S(1)}, u32[]{:S(2)}, u32[]{:S(2)}) collective-permute-start(s32[16,1]{0,1:T(1,128)S(1)} %get-tuple-element.137), channel_id=1, source_target_pairs={{0,3},{1,0},{2,1},{3,2},{4,7},{5,4},{6,5},{7,6},{8,11},{9,8},{10,9... | collective-permute-start | bytes 200 | tf_op jit(solution)/shard_map/while/body/eval_jaxpr/ppermute | solution.py:12
  175.8 10.2 %collective-permute-start.2 = (bf16[128,1024]{1,0:T(8,128)(2,1)S(1)}, bf16[128,1024]{1,0:T(8,128)(2,1)S(1)}, u32[]{:S(2)}, u32[]{:S(2)}) collective-permute-start(bf16[128,1024]{1,0:T(8,128)(2,1)S(1)} %copy.16), channel_id=1, source_target_pairs={{0,28},{4,0},{8,4},{12,8},{16,12},{20,16},{24,20},{28,24},{1,29},{... | collective-permute-start | bytes 786440 | tf_op jit(solution)/shard_map/while/body/eval_jaxpr/ppermute | solution.py:12
  175.9 10.1 %collective-permute-start.3 = (s32[1,8]{1,0:T(1,128)S(1)}, s32[1,8]{1,0:T(1,128)S(1)}, u32[]{:S(2)}, u32[]{:S(2)}) collective-permute-start(s32[1,8]{1,0:T(1,128)S(1)} %copy.17), channel_id=1, source_target_pairs={{0,28},{4,0},{8,4},{12,8},{16,12},{20,16},{24,20},{28,24},{1,29},{... | collective-permute-start | bytes 104 | tf_op jit(solution)/shard_map/while/body/eval_jaxpr/ppermute | solution.py:12
  186.1 12.9 %collective-permute-start = (bf16[2048,128]{1,0:T(8,128)(2,1)S(1)}, bf16[2048,128]{1,0:T(8,128)(2,1)S(1)}, u32[]{:S(2)}, u32[]{:S(2)}) collective-permute-start(bf16[2048,128]{1,0:T(8,128)(2,1)S(1)} %get-tuple-element.135), channel_id=1, source_target_pairs={{0,3},{1,0},{2,1},{3,2},{4,7},{5,4},{6,5},{7,6},{8,11},{9,8},{10,9... | collective-permute-start | bytes 1572872 | tf_op jit(solution)/shard_map/while/body/eval_jaxpr/ppermute | solution.py:12
  189.2 9.8 %collective-permute-start.1 = (s32[16,1]{0,1:T(1,128)S(1)}, s32[16,1]{0,1:T(1,128)S(1)}, u32[]{:S(2)}, u32[]{:S(2)}) collective-permute-start(s32[16,1]{0,1:T(1,128)S(1)} %get-tuple-element.137), channel_id=1, source_target_pairs={{0,3},{1,0},{2,1},{3,2},{4,7},{5,4},{6,5},{7,6},{8,11},{9,8},{10,9... | collective-permute-start | bytes 200 | tf_op jit(solution)/shard_map/while/body/eval_jaxpr/ppermute | solution.py:12
  189.3 9.9 %collective-permute-start.2 = (bf16[128,1024]{1,0:T(8,128)(2,1)S(1)}, bf16[128,1024]{1,0:T(8,128)(2,1)S(1)}, u32[]{:S(2)}, u32[]{:S(2)}) collective-permute-start(bf16[128,1024]{1,0:T(8,128)(2,1)S(1)} %copy.16), channel_id=1, source_target_pairs={{0,28},{4,0},{8,4},{12,8},{16,12},{20,16},{24,20},{28,24},{1,29},{... | collective-permute-start | bytes 786440 | tf_op jit(solution)/shard_map/while/body/eval_jaxpr/ppermute | solution.py:12
  189.3 9.8 %collective-permute-start.3 = (s32[1,8]{1,0:T(1,128)S(1)}, s32[1,8]{1,0:T(1,128)S(1)}, u32[]{:S(2)}, u32[]{:S(2)}) collective-permute-start(s32[1,8]{1,0:T(1,128)S(1)} %copy.17), channel_id=1, source_target_pairs={{0,28},{4,0},{8,4},{12,8},{16,12},{20,16},{24,20},{28,24},{1,29},{... | collective-permute-start | bytes 104 | tf_op jit(solution)/shard_map/while/body/eval_jaxpr/ppermute | solution.py:12
  228.2 2.2 copy-start
  231.0 3.6 %collective-permute-start.16 = (bf16[1,256,1024]{2,1,0:T(8,128)(2,1)S(1)}, bf16[1,256,1024]{2,1,0:T(8,128)(2,1)S(1)}, u32[]{:S(2)}, u32[]{:S(2)}) collective-permute-start(bf16[1,256,1024]{2,1,0:T(8,128)(2,1)S(1)} %get-tuple-element.90), channel_id=1, source_target_pairs={{0,4},{4,0},{8,12},{12,8},{16,20},{20,16},{24,28},{28,24},{1,5},{5... | collective-permute-start | bytes 1572872 | tf_op jit(solution)/shard_map/ppermute | solution.py:104
  231.1 14.8 %collective-permute-start.17 = (bf16[1,256,1024]{2,1,0:T(8,128)(2,1)S(1)}, bf16[1,256,1024]{2,1,0:T(8,128)(2,1)S(1)}, u32[]{:S(2)}, u32[]{:S(2)}) collective-permute-start(bf16[1,256,1024]{2,1,0:T(8,128)(2,1)S(1)} %get-tuple-element.89), channel_id=1, source_target_pairs={{0,8},{4,12},{8,0},{12,4},{16,24},{20,28},{24,16},{28,20},{1,9},{5... | collective-permute-start | bytes 1572872 | tf_op jit(solution)/shard_map/ppermute | solution.py:104
  231.9 24.3 %collective-permute-start.18 = (bf16[1,256,1024]{2,1,0:T(8,128)(2,1)S(1)}, bf16[1,256,1024]{2,1,0:T(8,128)(2,1)S(1)}, u32[]{:S(2)}, u32[]{:S(2)}) collective-permute-start(bf16[1,256,1024]{2,1,0:T(8,128)(2,1)S(1)} %get-tuple-element.88), channel_id=1, source_target_pairs={{0,12},{4,8},{8,4},{12,0},{16,28},{20,24},{24,20},{28,16},{1,13},{... | collective-permute-start | bytes 1572872 | tf_op jit(solution)/shard_map/ppermute | solution.py:104
  232.9 23.3 %collective-permute-start.19 = (bf16[1,256,1024]{2,1,0:T(8,128)(2,1)S(1)}, bf16[1,256,1024]{2,1,0:T(8,128)(2,1)S(1)}, u32[]{:S(2)}, u32[]{:S(2)}) collective-permute-start(bf16[1,256,1024]{2,1,0:T(8,128)(2,1)S(1)} %get-tuple-element.87), channel_id=1, source_target_pairs={{0,16},{4,20},{8,24},{12,28},{16,0},{20,4},{24,8},{28,12},{1,17},{... | collective-permute-start | bytes 1572872 | tf_op jit(solution)/shard_map/ppermute | solution.py:104
  233.8 46.5 %collective-permute-start.20 = (bf16[1,256,1024]{2,1,0:T(8,128)(2,1)S(1)}, bf16[1,256,1024]{2,1,0:T(8,128)(2,1)S(1)}, u32[]{:S(2)}, u32[]{:S(2)}) collective-permute-start(bf16[1,256,1024]{2,1,0:T(8,128)(2,1)S(1)} %get-tuple-element.86), channel_id=1, source_target_pairs={{0,20},{4,16},{8,28},{12,24},{16,4},{20,0},{24,12},{28,8},{1,21},{... | collective-permute-start | bytes 1572872 | tf_op jit(solution)/shard_map/ppermute | solution.py:104
  234.6 45.7 %collective-permute-start.21 = (bf16[1,256,1024]{2,1,0:T(8,128)(2,1)S(1)}, bf16[1,256,1024]{2,1,0:T(8,128)(2,1)S(1)}, u32[]{:S(2)}, u32[]{:S(2)}) collective-permute-start(bf16[1,256,1024]{2,1,0:T(8,128)(2,1)S(1)} %get-tuple-element.85), channel_id=1, source_target_pairs={{0,24},{4,28},{8,16},{12,20},{16,8},{20,12},{24,0},{28,4},{1,25},{... | collective-permute-start | bytes 1572872 | tf_op jit(solution)/shard_map/ppermute | solution.py:104
  245.9 34.5 %collective-permute-start.22 = (bf16[1,256,1024]{2,1,0:T(8,128)(2,1)S(1)}, bf16[1,256,1024]{2,1,0:T(8,128)(2,1)S(1)}, u32[]{:S(2)}, u32[]{:S(2)}) collective-permute-start(bf16[1,256,1024]{2,1,0:T(8,128)(2,1)S(1)} %get-tuple-element.84), channel_id=1, source_target_pairs={{0,28},{4,24},{8,20},{12,16},{16,12},{20,8},{24,4},{28,0},{1,29},{... | collective-permute-start | bytes 1572872 | tf_op jit(solution)/shard_map/ppermute | solution.py:104
  (1 other events, 2.0 us)
